TPU v7x, 32 devices: a whole 2x2x4 slice. The times are simulated.
32 devices in a mesh: lat: 4 (over y, x), lon: 8 (over z, core).
Axes of the slice: x: 2, y: 2, z: 4, core: 2. Of those that a mesh axis runs over, the one named last changes fastest.
Arguments:
- inputs: bfloat16 [360, 360, 256], P('lat', 'lon'), may hold values from -6 to 6
- kernel: bfloat16 [3, 3, 256, 256], replicated, may hold values from -0.125 to 0.125
- cotangent: bfloat16 [360, 360, 256], P('lat', 'lon'), may hold values from -6 to 6
Outputs:
- outputs: bfloat16 [360, 360, 256], P('lat', 'lon')
- input_grad: bfloat16 [360, 360, 256], P('lat', 'lon')
- kernel_grad: float32 [3, 3, 256, 256], replicated
All inputs are finite; a program needn't handle non-finite values.
Results may differ from a plain program's by a relative error of at most 0.001.
Values may be sent and summed in bfloat16 or wider, within the bound.
No kernel may reach another device: no remote copies, remote signals or barrier semaphores. Data moves between devices by JAX's collectives and lax.ppermute only.
A program may use at most 192 MiB of HBM per device.

v0:
```python
import math
import jax
import jax.numpy as jnp
from jax import lax
from jax.sharding import PartitionSpec as P


def with_halo(cells, sides, width):
    for axis, dim in sides:
        count = lax.axis_size(axis)
        head = lax.slice_in_dim(cells, 0, width, axis=dim)
        tail = lax.slice_in_dim(cells, cells.shape[dim] - width, cells.shape[dim], axis=dim)
        cells = jnp.concatenate(
            [
                lax.ppermute(tail, axis, [(i, (i + 1) % count) for i in range(count)]),
                cells,
                lax.ppermute(head, axis, [((i + 1) % count, i) for i in range(count)]),
            ],
            axis=dim,
        )
    return cells


def from_behind(value, axis, steps):
    count = lax.axis_size(axis)
    pairs = [(source, (source + steps) % count) for source in range(count)]
    return lax.ppermute(value, axis, pairs)


def patches(padded, rows, cols):
    pieces = [
        padded[row_tap : row_tap + rows, col_tap : col_tap + cols]
        for row_tap in range(3)
        for col_tap in range(3)
    ]
    return jnp.concatenate(pieces, axis=-1).reshape(rows * cols, -1)


def surround(field):
    return with_halo(field, (("lat", 0), ("lon", 1)), 1)


def polar(padded):
    both = jnp.stack([padded[1], padded[-2]])
    moved = from_behind(both, "lon", lax.axis_size("lon") // 2)
    return (moved[0], moved[1])


def edge_term(row_data, weights, cols, width):
    stacked = jnp.concatenate([row_data[offset : offset + cols] for offset in range(3)], axis=-1)
    return jnp.dot(stacked, weights.reshape(-1, width), preferred_element_type=jnp.float32)


def local(inputs, kernel, cotangent):
    rows, cols, width = inputs.shape
    north = lax.axis_index("lat") == 0
    south = lax.axis_index("lat") == lax.axis_size("lat") - 1
    padded = surround(inputs)
    top, bottom = polar(padded)
    padded = jnp.concatenate(
        [
            jnp.where(north, top, padded[0])[None],
            padded[1:-1],
            jnp.where(south, bottom, padded[-1])[None],
        ],
        0,
    )
    columns = patches(padded, rows, cols)
    outputs = jnp.dot(columns, kernel.reshape(-1, width), preferred_element_type=jnp.float32)
    outputs = outputs.reshape(rows, cols, width).astype(jnp.bfloat16)
    flat_grad = cotangent.reshape(-1, width)
    local_grad = lax.dot_general(
        columns, flat_grad, (((0,), (0,)), ((), ())), preferred_element_type=jnp.float32
    )
    local_grad = local_grad.reshape(3, 3, width, width)
    padded_grad = surround(cotangent)
    grad_top, grad_bottom = polar(padded_grad)
    empty_row = jnp.zeros_like(padded_grad[0])
    padded_grad = jnp.concatenate(
        [
            jnp.where(north, empty_row, padded_grad[0])[None],
            padded_grad[1:-1],
            jnp.where(south, empty_row, padded_grad[-1])[None],
        ],
        0,
    )
    flipped = jnp.transpose(kernel[::-1, ::-1], (0, 1, 3, 2))
    input_grad = jnp.dot(
        patches(padded_grad, rows, cols),
        flipped.reshape(-1, width),
        preferred_element_type=jnp.float32,
    )
    input_grad = input_grad.reshape(rows, cols, width)
    north_term = edge_term(grad_top, flipped[2], cols, width)
    south_term = edge_term(grad_bottom, flipped[0], cols, width)
    input_grad = input_grad.at[0].add(jnp.where(north, north_term, 0.0))
    input_grad = input_grad.at[-1].add(jnp.where(south, south_term, 0.0))
    factor = 1.0 / math.sqrt(rows * cols * lax.axis_size("lat") * lax.axis_size("lon"))
    partial_sum = lax.psum(local_grad, "lon")
    summed = lax.psum(partial_sum, "lat")
    return (outputs, input_grad.astype(jnp.bfloat16), summed * factor)


def solution(mesh):
    in_specs = (P("lat", "lon", None), P(), P("lat", "lon", None))
    out_specs = (P("lat", "lon", None), P("lat", "lon", None), P())
    return jax.shard_map(local, mesh=mesh, in_specs=in_specs, out_specs=out_specs, check_vma=False)
```

profile of v0, /device:TPU:0, one launch (start us, length us, event | category | flops | bytes accessed | tf_op | source)
XLA Modules:
  0.0 271.3 jit_solution(15557798716294932809)
XLA Ops:
  8.0 3.9 %collective-permute-start.1 = (bf16[1,45,256]{2,1,0:T(8,128)(2,1)S(1)}, bf16[1,45,256]{2,1,0:T(8,128)(2,1)S(1)}, u32[]{:S(2)}, u32[]{:S(2)}) collective-permute-start(bf16[1,45,256]{2,1,0:T(8,128)(2,1)S(1)} %get-tuple-element.37), channel_id=1, source_target_pairs={{8,0},{16,8},{24,16},{0,24},{9,1},{17,9},{25,17},{1,25},{10,2},{18... | collective-permute-start | bytes 69128 | tf_op jit(solution)/shard_map/ppermute | solution.py:17
  13.3 2.9 %collective-permute-start.6 = (bf16[1,45,256]{2,1,0:T(8,128)(2,1)}, bf16[1,45,256]{2,1,0:T(8,128)(2,1)S(1)}, u32[]{:S(2)}, u32[]{:S(2)}) collective-permute-start(bf16[1,45,256]{2,1,0:T(8,128)(2,1)} %get-tuple-element.35), channel_id=1, source_target_pairs={{8,0},{16,8},{24,16},{0,24},{9,1},{17,9},{25,17},{1,25},{10,2},{18... | collective-permute-start | bytes 69128 | tf_op jit(solution)/shard_map/ppermute | solution.py:17
  19.9 1.9 reshape.103
  22.2 3.5 %collective-permute-start.8 = (bf16[92,1,256]{2,1,0:T(2,128)(2,1)S(1)}, bf16[92,1,256]{2,1,0:T(2,128)(2,1)S(1)}, u32[]{:S(2)}, u32[]{:S(2)}) collective-permute-start(bf16[92,1,256]{2,1,0:T(2,128)(2,1)S(1)} %get-tuple-element.32), channel_id=1, source_target_pairs={{1,0},{2,1},{3,2},{4,3},{5,4},{6,5},{7,6},{0,7},{9,8},{10,9},{11,1... | collective-permute-start | bytes 141320 | tf_op jit(solution)/shard_map/ppermute | solution.py:17
  26.2 3.5 %collective-permute-start.3 = (bf16[92,1,256]{2,1,0:T(2,128)(2,1)S(1)}, bf16[92,1,256]{2,1,0:T(2,128)(2,1)S(1)}, u32[]{:S(2)}, u32[]{:S(2)}) collective-permute-start(bf16[92,1,256]{2,1,0:T(2,128)(2,1)S(1)} %get-tuple-element.34), channel_id=1, source_target_pairs={{1,0},{2,1},{3,2},{4,3},{5,4},{6,5},{7,6},{0,7},{9,8},{10,9},{11,1... | collective-permute-start | bytes 141320 | tf_op jit(solution)/shard_map/ppermute | solution.py:17
  29.8 2.6 collective-permute-done.2
  34.6 1.6 fusion.7
  36.2 2.8 %fusion.5 = bf16[90,45,2304]{2,1,0:T(8,128)(2,1)} fusion(bf16[90,45,2304]{2,1,0:T(8,128)(2,1)} %fusion.7, bf16[1,47,256]{2,1,0:T(8,128)(2,1)S(1)} %get-tuple-element.30, bf16[90,47,256]{2,1,0:T(8,128)(2,1)S(1)} %slice.295), kind=kLoop, calls=%fused_computation.15 | loop fusion | flops 4147200 | bytes 4401664
  40.7 1.7 fusion.15
  42.5 2.7 %fusion.13 = bf16[90,45,2304]{2,1,0:T(8,128)(2,1)} fusion(bf16[90,45,2304]{2,1,0:T(8,128)(2,1)} %fusion.15, bf16[1,47,256]{2,1,0:T(8,128)(2,1)S(1)} %get-tuple-element.28, bf16[90,47,256]{2,1,0:T(8,128)(2,1)S(1)} %slice.283), kind=kLoop, calls=%fused_computation.23 | loop fusion | flops 4147200 | bytes 4401664
  45.2 2.8 %fusion.23 = bf16[90,45,2304]{2,1,0:T(8,128)(2,1)} fusion(bf16[90,45,2304]{2,1,0:T(8,128)(2,1)} %fusion.13, bf16[90,47,256]{2,1,0:T(8,128)(2,1)S(1)} %slice.283, bf16[1,47,256]{2,1,0:T(8,128)(2,1)S(1)} %get-tuple-element.28), kind=kLoop, calls=%fused_computation.41 | loop fusion | flops 4147200 | bytes 4401664
  48.0 2.9 %fusion.22 = bf16[90,45,2304]{2,1,0:T(8,128)(2,1)} fusion(bf16[90,45,2304]{2,1,0:T(8,128)(2,1)} %fusion.23, bf16[92,45,256]{2,1,0:T(8,128)(2,1)S(1)} %constant_dynamic-update-slice_fusion, bf16[92,1,256]{2,1,0:T(2,128)(2,1)S(1)} %collective-permute-done.2), kind=kLoop, calls=%fused_computation.39 | loop fusion | flops 4147200 | bytes 4378624
  50.8 1.7 constant_dynamic-update-slice_fusion.3
  52.5 3.1 %fusion.21 = bf16[90,45,2304]{2,1,0:T(8,128)(2,1)} fusion(bf16[90,45,2304]{2,1,0:T(8,128)(2,1)} %constant_dynamic-update-slice_fusion.3, bf16[92,1,256]{2,1,0:T(2,128)(2,1)S(1)} %collective-permute-done.3, bf16[92,45,256]{2,1,0:T(8,128)(2,1)S(1)} %constant_dynamic-update-slice_fusion), kind=kLoop, calls=%fused_computation.37 | loop fusion | flops 4147200 | bytes 4378624
  55.6 1.7 fusion.11
  57.3 2.8 %fusion.9 = bf16[90,45,2304]{2,1,0:T(8,128)(2,1)} fusion(bf16[90,45,2304]{2,1,0:T(8,128)(2,1)} %fusion.11, bf16[1,47,256]{2,1,0:T(8,128)(2,1)S(1)} %get-tuple-element.27, bf16[90,47,256]{2,1,0:T(8,128)(2,1)S(1)} %slice.283), kind=kLoop, calls=%fused_computation.19 | loop fusion | flops 4147200 | bytes 4401664
  60.0 3.1 %fusion.20 = bf16[90,45,2304]{2,1,0:T(8,128)(2,1)} fusion(bf16[90,45,2304]{2,1,0:T(8,128)(2,1)} %fusion.9, bf16[1,47,256]{2,1,0:T(8,128)(2,1)S(1)} %get-tuple-element.27, bf16[90,47,256]{2,1,0:T(8,128)(2,1)S(1)} %slice.283), kind=kLoop, calls=%fused_computation.35 | loop fusion | flops 4147200 | bytes 4401664 | tf_op jit(solution)/shard_map/concatenate | solution.py:36
  63.2 19.5 %reshape.99 = bf16[4050,2304]{1,0:T(8,128)(2,1)} reshape(bf16[90,45,2304]{2,1,0:T(8,128)(2,1)} %fusion.20) | data formatting | bytes 37324800 | tf_op jit(solution)/shard_map/reshape | solution.py:36
  82.7 23.0 %copy.7 = bf16[4050,2304]{0,1:T(8,128)(2,1)} copy(bf16[4050,2304]{1,0:T(8,128)(2,1)} %reshape.99) | data formatting | bytes 37324800 | tf_op jit(solution)/shard_map/reshape | solution.py:36
  105.7 10.6 %fusion.24 = f32[3,3,256,256]{3,2,1,0:T(8,128)} fusion(bf16[3,3,256,4050]{3,2,1,0:T(8,128)(2,1)} %bitcast.46, bf16[4050,256,1,1]{1,0,2,3:T(8,128)(2,1)} %reshape.103), kind=kOutput, calls=%fused_computation.42 | convolution fusion | flops 4777574400 | bytes 23095296 | tf_op jit(solution)/shard_map/dot_general | solution.py:72
  116.4 2.7 fusion.19
  119.1 2.8 %fusion.18 = bf16[90,45,2304]{2,1,0:T(8,128)(2,1)} fusion(bf16[90,45,2304]{2,1,0:T(8,128)(2,1)} %fusion.19, bf16[92,45,256]{2,1,0:T(8,128)(2,1)S(1)} %copy-done.1, bf16[92,1,256]{2,1,0:T(2,128)(2,1)S(1)} %collective-permute-done.7), kind=kLoop, calls=%fused_computation.31 | loop fusion | flops 4147200 | bytes 4378624
  121.9 1.6 constant_dynamic-update-slice_fusion.7
  123.4 2.9 %fusion.17 = bf16[90,45,2304]{2,1,0:T(8,128)(2,1)} fusion(bf16[90,45,2304]{2,1,0:T(8,128)(2,1)} %constant_dynamic-update-slice_fusion.7, bf16[92,1,256]{2,1,0:T(2,128)(2,1)S(1)} %collective-permute-done.8, bf16[92,45,256]{2,1,0:T(8,128)(2,1)S(1)} %copy-done.1), kind=kLoop, calls=%fused_computation.29 | loop fusion | flops 4147200 | bytes 4378624
  127.9 2.7 %fusion.1 = bf16[90,45,2304]{2,1,0:T(8,128)(2,1)} fusion(bf16[90,45,2304]{2,1,0:T(8,128)(2,1)} %fusion.3, bf16[1,47,256]{2,1,0:T(8,128)(2,1)S(1)} %get-tuple-element.29, bf16[90,47,256]{2,1,0:T(8,128)(2,1)S(1)} %slice.295), kind=kLoop, calls=%fused_computation.11 | loop fusion | flops 4147200 | bytes 4401664
  130.7 2.7 fusion.16
  133.4 51.7 %all-reduce.3.cloned.1.call-done = f32[3,3,256,256]{3,2,1,0:T(8,128)} async-done(((f32[3,3,256,256]{3,2,1,0:T(8,128)}), f32[3,3,256,256]{3,2,1,0:T(8,128)}) %all-reduce.3.cloned.1.call-update) | async-done | bytes 2359312 | tf_op jit(solution)/shard_map/psum | solution.py:99
  185.2 9.9 %fusion.72 = f32[90,45,256]{2,1,0:T(8,128)S(1)} fusion(bf16[90,45,2304]{2,1,0:T(8,128)(2,1)} %fusion.16, bf16[2304,256,1]{1,0,2:T(8,128)(2,1)S(1)} %bitcast.50), kind=kOutput, calls=%fused_computation.114 | convolution fusion | flops 4777574400 | bytes 23989248 | tf_op jit(solution)/shard_map/dot_general | solution.py:88
  195.6 1.6 convert_element_type.7
  197.2 11.6 %convolution_convert_fusion = bf16[90,45,256]{2,1,0:T(8,128)(2,1)} fusion(bf16[90,45,2304]{2,1,0:T(8,128)(2,1)} %fusion.20, bf16[2304,256,1]{1,0,2:T(8,128)(2,1)S(1)} %bitcast.49), kind=kOutput, calls=%fused_computation.44 | convolution fusion | flops 4778611200 | bytes 21915648 | tf_op jit(solution)/shard_map/dot_general | solution.py:69
  208.8 52.4 %all-reduce.5.cloned.1.call-done = f32[3,3,256,256]{3,2,1,0:T(8,128)} async-done(((f32[3,3,256,256]{3,2,1,0:T(8,128)}), f32[3,3,256,256]{3,2,1,0:T(8,128)}) %all-reduce.5.cloned.1.call-update) | async-done | bytes 2359312 | tf_op jit(solution)/shard_map/psum | solution.py:100
  261.2 3.3 %broadcast_multiply_fusion = f32[3,3,256,256]{3,2,1,0:T(8,128)} fusion(f32[3,3,256,256]{3,2,1,0:T(8,128)} %all-reduce.5.cloned.1.call-done), kind=kLoop, calls=%fused_computation.45 | loop fusion | flops 589824 | bytes 4718592 | tf_op jit(solution)/shard_map/mul | solution.py:101
  (63 shorter events, 12.7 us)
Async XLA Ops:
  7.2 178.0 %all-reduce.3.cloned.1.call-start = ((), (), s32[]{:S(2)}) async-start(), calls=%async_computation | async-start | bytes 4718592 | tf_op jit(solution)/shard_map/psum | solution.py:99
  8.0 18.0 %collective-permute-start.1 = (bf16[1,45,256]{2,1,0:T(8,128)(2,1)S(1)}, bf16[1,45,256]{2,1,0:T(8,128)(2,1)S(1)}, u32[]{:S(2)}, u32[]{:S(2)}) collective-permute-start(bf16[1,45,256]{2,1,0:T(8,128)(2,1)S(1)} %get-tuple-element.37), channel_id=1, source_target_pairs={{8,0},{16,8},{24,16},{0,24},{9,1},{17,9},{25,17},{1,25},{10,2},{18... | collective-permute-start | bytes 69128 | tf_op jit(solution)/shard_map/ppermute | solution.py:17
  11.9 13.9 %collective-permute-start = (bf16[1,45,256]{2,1,0:T(8,128)(2,1)S(1)}, bf16[1,45,256]{2,1,0:T(8,128)(2,1)S(1)}, u32[]{:S(2)}, u32[]{:S(2)}) collective-permute-start(bf16[1,45,256]{2,1,0:T(8,128)(2,1)S(1)} %get-tuple-element.38), channel_id=1, source_target_pairs={{0,8},{8,16},{16,24},{24,0},{1,9},{9,17},{17,25},{25,1},{2,10},{10... | collective-permute-start | bytes 69128 | tf_op jit(solution)/shard_map/ppermute | solution.py:15
  13.3 8.7 %collective-permute-start.6 = (bf16[1,45,256]{2,1,0:T(8,128)(2,1)}, bf16[1,45,256]{2,1,0:T(8,128)(2,1)S(1)}, u32[]{:S(2)}, u32[]{:S(2)}) collective-permute-start(bf16[1,45,256]{2,1,0:T(8,128)(2,1)} %get-tuple-element.35), channel_id=1, source_target_pairs={{8,0},{16,8},{24,16},{0,24},{9,1},{17,9},{25,17},{1,25},{10,2},{18... | collective-permute-start | bytes 69128 | tf_op jit(solution)/shard_map/ppermute | solution.py:17
  16.2 5.6 %collective-permute-start.5 = (bf16[1,45,256]{2,1,0:T(8,128)(2,1)}, bf16[1,45,256]{2,1,0:T(8,128)(2,1)S(1)}, u32[]{:S(2)}, u32[]{:S(2)}) collective-permute-start(bf16[1,45,256]{2,1,0:T(8,128)(2,1)} %get-tuple-element.36), channel_id=1, source_target_pairs={{0,8},{8,16},{16,24},{24,0},{1,9},{9,17},{17,25},{25,1},{2,10},{10... | collective-permute-start | bytes 69128 | tf_op jit(solution)/shard_map/ppermute | solution.py:15
  17.9 2.0 copy-start.2
  21.8 4.0 %copy-start.4 = (bf16[90,45,256]{2,1,0:T(8,128)(2,1)S(1)}, bf16[90,45,256]{2,1,0:T(8,128)(2,1)}, u32[]{:S(2)}) copy-start(bf16[90,45,256]{2,1,0:T(8,128)(2,1)} %param.7) | copy-start | bytes 6220804
  22.0 12.5 %copy-start = (bf16[92,45,256]{2,1,0:T(8,128)(2,1)}, bf16[92,45,256]{2,1,0:T(8,128)(2,1)S(1)}, u32[]{:S(2)}) copy-start(bf16[92,45,256]{2,1,0:T(8,128)(2,1)S(1)} %constant_dynamic-update-slice_fusion.4) | copy-start | bytes 6359044
  22.2 7.5 %collective-permute-start.7 = (bf16[92,1,256]{2,1,0:T(2,128)(2,1)S(1)}, bf16[92,1,256]{2,1,0:T(2,128)(2,1)S(1)}, u32[]{:S(2)}, u32[]{:S(2)}) collective-permute-start(bf16[92,1,256]{2,1,0:T(2,128)(2,1)S(1)} %get-tuple-element.31), channel_id=1, source_target_pairs={{0,1},{1,2},{2,3},{3,4},{4,5},{5,6},{6,7},{7,0},{8,9},{9,10},{10,1... | collective-permute-start | bytes 141320 | tf_op jit(solution)/shard_map/ppermute | solution.py:15
  22.2 7.5 %collective-permute-start.8 = (bf16[92,1,256]{2,1,0:T(2,128)(2,1)S(1)}, bf16[92,1,256]{2,1,0:T(2,128)(2,1)S(1)}, u32[]{:S(2)}, u32[]{:S(2)}) collective-permute-start(bf16[92,1,256]{2,1,0:T(2,128)(2,1)S(1)} %get-tuple-element.32), channel_id=1, source_target_pairs={{1,0},{2,1},{3,2},{4,3},{5,4},{6,5},{7,6},{0,7},{9,8},{10,9},{11,1... | collective-permute-start | bytes 141320 | tf_op jit(solution)/shard_map/ppermute | solution.py:17
  26.1 6.3 %collective-permute-start.2 = (bf16[92,1,256]{2,1,0:T(2,128)(2,1)S(1)}, bf16[92,1,256]{2,1,0:T(2,128)(2,1)S(1)}, u32[]{:S(2)}, u32[]{:S(2)}) collective-permute-start(bf16[92,1,256]{2,1,0:T(2,128)(2,1)S(1)} %get-tuple-element.33), channel_id=1, source_target_pairs={{0,1},{1,2},{2,3},{3,4},{4,5},{5,6},{6,7},{7,0},{8,9},{9,10},{10,1... | collective-permute-start | bytes 141320 | tf_op jit(solution)/shard_map/ppermute | solution.py:15
  26.2 6.2 %collective-permute-start.3 = (bf16[92,1,256]{2,1,0:T(2,128)(2,1)S(1)}, bf16[92,1,256]{2,1,0:T(2,128)(2,1)S(1)}, u32[]{:S(2)}, u32[]{:S(2)}) collective-permute-start(bf16[92,1,256]{2,1,0:T(2,128)(2,1)S(1)} %get-tuple-element.34), channel_id=1, source_target_pairs={{1,0},{2,1},{3,2},{4,3},{5,4},{6,5},{7,6},{0,7},{9,8},{10,9},{11,1... | collective-permute-start | bytes 141320 | tf_op jit(solution)/shard_map/ppermute | solution.py:17
  29.8 165.3 %collective-permute-start.9 = (bf16[2,47,256]{2,1,0:T(8,128)(2,1)S(1)}, bf16[2,47,256]{2,1,0:T(8,128)(2,1)S(1)}, u32[]{:S(2)}, u32[]{:S(2)}) collective-permute-start(bf16[2,47,256]{2,1,0:T(8,128)(2,1)S(1)} %fusion.57), channel_id=1, source_target_pairs={{0,4},{1,5},{2,6},{3,7},{4,0},{5,1},{6,2},{7,3},{8,12},{9,13},{10,... | collective-permute-start | bytes 144392 | tf_op jit(solution)/shard_map/ppermute | solution.py:27
  32.4 8.3 %collective-permute-start.4 = (bf16[2,47,256]{2,1,0:T(8,128)(2,1)S(1)}, bf16[2,47,256]{2,1,0:T(8,128)(2,1)S(1)}, u32[]{:S(2)}, u32[]{:S(2)}) collective-permute-start(bf16[2,47,256]{2,1,0:T(8,128)(2,1)S(1)} %fusion.54), channel_id=1, source_target_pairs={{0,4},{1,5},{2,6},{3,7},{4,0},{5,1},{6,2},{7,3},{8,12},{9,13},{10,... | collective-permute-start | bytes 144392 | tf_op jit(solution)/shard_map/ppermute | solution.py:27
  116.3 144.9 %all-reduce.5.cloned.1.call-start = ((), (), s32[]{:S(2)}) async-start(), calls=%async_computation.1 | async-start | bytes 4718592 | tf_op jit(solution)/shard_map/psum | solution.py:100
  116.4 2.7 %copy-start.1 = (bf16[92,45,256]{2,1,0:T(8,128)(2,1)S(1)}, bf16[92,45,256]{2,1,0:T(8,128)(2,1)}, u32[]{:S(2)}) copy-start(bf16[92,45,256]{2,1,0:T(8,128)(2,1)} %copy-done) | copy-start | bytes 6359044
  119.1 2.8 %copy-start.3 = (bf16[90,45,256]{2,1,0:T(8,128)(2,1)S(1)}, bf16[90,45,256]{2,1,0:T(8,128)(2,1)}, u32[]{:S(2)}) copy-start(bf16[90,45,256]{2,1,0:T(8,128)(2,1)} %param.9) | copy-start | bytes 6220804
  133.4 51.8 %copy-start.8 = (bf16[3,3,256,256]{2,3,1,0:T(8,128)(2,1)S(1)}, bf16[3,3,256,256]{2,3,1,0:T(8,128)(2,1)}, u32[]{:S(2)}) copy-start(bf16[3,3,256,256]{2,3,1,0:T(8,128)(2,1)} %rev.3) | copy-start | bytes 3538948
  185.2 9.9 %copy-start.6 = (bf16[1,3,256,256]{3,2,1,0:T(8,128)(2,1)S(1)}, bf16[1,3,256,256]{3,2,1,0:T(8,128)(2,1)}, u32[]{:S(2)}) copy-start(bf16[1,3,256,256]{3,2,1,0:T(8,128)(2,1)} %get-tuple-element.40) | copy-start | bytes 1179652
  185.2 10.2 %copy-start.5 = (bf16[1,3,256,256]{3,2,1,0:T(8,128)(2,1)S(1)}, bf16[1,3,256,256]{3,2,1,0:T(8,128)(2,1)}, u32[]{:S(2)}) copy-start(bf16[1,3,256,256]{3,2,1,0:T(8,128)(2,1)} %get-tuple-element.39) | copy-start | bytes 1179652
  195.5 1.6 copy-start.7
Sparse Core Ops, SparseCore 0:
  116.4 68.6 all-reduce.2
  188.3 72.8 all-reduce.4
where the time goes:
time: 272 us; the launch traced here: 271 us
  waiting for transfers between devices  107 us (39%)
  local copies, waits for them, and re-layouts  54.5 us (20%)
  other arithmetic  48.6 us (18%)
  matrix products  32.5 us (12%)
  starting transfers between devices  14.6 us (5%)
  between operations  14.3 us (5%)
    psum x1, waiting for transfers between devices, local(): summed = lax.psum(partial_sum, 'lat')  52.4 us
    psum x1, waiting for transfers between devices, local(): partial_sum = lax.psum(local_grad, 'lon')  51.7 us
    reshape x2, local copies, waits for them, and re-layouts, patches(): return jnp.concatenate(pieces, axis=-1).reshape(rows * cols, -1)  42.5 us
    unnamed x14, other arithmetic  34.7 us
    ppermute x4, starting transfers between devices, with_halo(): lax.ppermute(head, axis, [((i + 1) % count, i) for i in range(count)])  13.9 us
    dot_general x1, matrix products, local(): jnp.dot(columns, kernel.reshape(-1, width), preferred_element_type=jnp.fl...  11.6 us
    dot_general x1, matrix products, local(): lax.dot_general(columns, flat_grad, (((0,), (0,)), ((), ())), preferred_e...  10.6 us
    dot_general x1, matrix products, local(): jnp.dot(patches(padded_grad, rows, cols), flipped.reshape(-1, width), pre...  9.87 us
  transfers between devices with their start and end apart: 12, of which 3 were waited for; matrix products, arithmetic and copies ran while one was open for 48% of the time, Pallas kernels for 0%

commit v1 on v0

--- a/solution.py
+++ b/solution.py
@@ -97,7 +97,9 @@
     input_grad = input_grad.at[-1].add(jnp.where(south, south_term, 0.0))
     factor = 1.0 / math.sqrt(rows * cols * lax.axis_size("lat") * lax.axis_size("lon"))
     partial_sum = lax.psum(local_grad, "lon")
-    summed = lax.psum(partial_sum, "lat")
+    summed = partial_sum
+    for hop in (1, 2):
+        summed = summed + lax.ppermute(summed, "lat", [(dev, dev ^ hop) for dev in range(4)])
     return (outputs, input_grad.astype(jnp.bfloat16), summed * factor)
 
 

time: 272 us -> 286 us (1.051)
  local copies, waits for them, and re-layouts: 54.5 us -> 63 us
  other arithmetic: 48.6 us -> 51.8 us
  starting transfers between devices: 14.6 us -> 17.7 us
    psum x1 -> x0, waiting for transfers between devices: 52.4 us -> none  [local(): summed = lax.psum(partial_sum, 'lat')]
    ppermute x0 -> x2, waiting for transfers between devices: none -> 41.6 us  [local(): lax.ppermute(summed, 'lat', [(dev, dev ^ hop) for dev in range(4)])]
    psum x1, waiting for transfers between devices: 51.7 us -> 57.1 us  [local(): partial_sum = lax.psum(local_grad, 'lon')]
    ppermute x4, starting transfers between devices: 13.9 us -> 9.99 us  [with_halo(): lax.ppermute(head, axis, [((i + 1) % count, i) for i in range(count)])]
    ppermute x4, starting transfers between devices: 0.12 us -> 3.13 us  [with_halo(): lax.ppermute(tail, axis, [(i, (i + 1) % count) for i in range(count)])]
    ppermute x0 -> x2, starting transfers between devices: none -> 2.98 us  [local(): lax.ppermute(summed, 'lat', [(dev, dev ^ hop) for dev in range(4)])]
  transfers between devices with their start and end apart: 12 -> 13, of which waited for: 3 -> 7; matrix products, arithmetic and copies ran while one was open for 48% -> 24% of each run, Pallas kernels for 0% -> 0%
where the time goes in v1:
time: 286 us; the launch traced here: 285 us
  waiting for transfers between devices  106 us (37%)
  local copies, waits for them, and re-layouts  63 us (22%)
  other arithmetic  51.8 us (18%)
  matrix products  32.2 us (11%)
  starting transfers between devices  17.7 us (6%)
  between operations  14.2 us (5%)
    psum x1, waiting for transfers between devices, local(): partial_sum = lax.psum(local_grad, 'lon')  57.1 us
    reshape x2, local copies, waits for them, and re-layouts, patches(): return jnp.concatenate(pieces, axis=-1).reshape(rows * cols, -1)  44.3 us
    ppermute x2, waiting for transfers between devices, local(): lax.ppermute(summed, 'lat', [(dev, dev ^ hop) for dev in range(4)])  41.6 us
    unnamed x14, other arithmetic  35.6 us
    dot_general x1, matrix products, local(): jnp.dot(columns, kernel.reshape(-1, width), preferred_element_type=jnp.fl...  11.5 us
    dot_general x1, matrix products, local(): lax.dot_general(columns, flat_grad, (((0,), (0,)), ((), ())), preferred_e...  10.4 us
    ppermute x4, starting transfers between devices, with_halo(): lax.ppermute(head, axis, [((i + 1) % count, i) for i in range(count)])  9.99 us
    dot_general x1, matrix products, local(): jnp.dot(patches(padded_grad, rows, cols), flipped.reshape(-1, width), pre...  9.85 us
  transfers between devices with their start and end apart: 13, of which 7 were waited for; matrix products, arithmetic and copies ran while one was open for 24% of the time, Pallas kernels for 0%

profile of v1, /device:TPU:0, one launch (start us, length us, event | category | flops | bytes accessed | tf_op | source)
XLA Modules:
  0.0 284.9 jit_solution(6198679087887600608)
XLA Ops:
  8.0 3.0 %collective-permute-start = (bf16[1,45,256]{2,1,0:T(8,128)(2,1)S(1)}, bf16[1,45,256]{2,1,0:T(8,128)(2,1)S(1)}, u32[]{:S(2)}, u32[]{:S(2)}) collective-permute-start(bf16[1,45,256]{2,1,0:T(8,128)(2,1)S(1)} %get-tuple-element.38), channel_id=1, source_target_pairs={{0,8},{8,16},{16,24},{24,0},{1,9},{9,17},{17,25},{25,1},{2,10},{10... | collective-permute-start | bytes 69128 | tf_op jit(solution)/shard_map/ppermute | solution.py:15
  13.7 1.8 constant_dynamic-update-slice_fusion.1
  15.7 3.5 %collective-permute-start.3 = (bf16[92,1,256]{2,1,0:T(2,128)(2,1)S(1)}, bf16[92,1,256]{2,1,0:T(2,128)(2,1)S(1)}, u32[]{:S(2)}, u32[]{:S(2)}) collective-permute-start(bf16[92,1,256]{2,1,0:T(2,128)(2,1)S(1)} %get-tuple-element.34), channel_id=1, source_target_pairs={{1,0},{2,1},{3,2},{4,3},{5,4},{6,5},{7,6},{0,7},{9,8},{10,9},{11,1... | collective-permute-start | bytes 141320 | tf_op jit(solution)/shard_map/ppermute | solution.py:17
  19.2 4.0 %reshape.103 = bf16[4050,256,1,1]{1,0,2,3:T(8,128)(2,1)} reshape(bf16[90,45,256]{2,1,0:T(8,128)(2,1)} %param.9) | data formatting | bytes 4147200 | tf_op jit(solution)/shard_map/reshape | solution.py:71
  26.4 2.3 collective-permute-done.4
  30.4 2.8 %fusion.13 = bf16[90,45,2304]{2,1,0:T(8,128)(2,1)} fusion(bf16[90,45,2304]{2,1,0:T(8,128)(2,1)} %fusion.15, bf16[1,47,256]{2,1,0:T(8,128)(2,1)S(1)} %get-tuple-element.28, bf16[90,47,256]{2,1,0:T(8,128)(2,1)S(1)} %slice.283), kind=kLoop, calls=%fused_computation.24 | loop fusion | flops 4147200 | bytes 4401664
  33.3 2.8 fusion.23
  36.0 2.9 %fusion.22 = bf16[90,45,2304]{2,1,0:T(8,128)(2,1)} fusion(bf16[90,45,2304]{2,1,0:T(8,128)(2,1)} %fusion.23, bf16[92,45,256]{2,1,0:T(8,128)(2,1)S(1)} %constant_dynamic-update-slice_fusion, bf16[92,1,256]{2,1,0:T(2,128)(2,1)S(1)} %collective-permute-done.2), kind=kLoop, calls=%fused_computation.40 | loop fusion | flops 4147200 | bytes 4378624
  40.7 2.9 %fusion.21 = bf16[90,45,2304]{2,1,0:T(8,128)(2,1)} fusion(bf16[90,45,2304]{2,1,0:T(8,128)(2,1)} %constant_dynamic-update-slice_fusion.3, bf16[92,1,256]{2,1,0:T(2,128)(2,1)S(1)} %collective-permute-done.3, bf16[92,45,256]{2,1,0:T(8,128)(2,1)S(1)} %constant_dynamic-update-slice_fusion), kind=kLoop, calls=%fused_computation.38 | loop fusion | flops 4147200 | bytes 4378624
  45.2 2.9 %fusion.9 = bf16[90,45,2304]{2,1,0:T(8,128)(2,1)} fusion(bf16[90,45,2304]{2,1,0:T(8,128)(2,1)} %fusion.11, bf16[1,47,256]{2,1,0:T(8,128)(2,1)S(1)} %get-tuple-element.27, bf16[90,47,256]{2,1,0:T(8,128)(2,1)S(1)} %slice.283), kind=kLoop, calls=%fused_computation.20 | loop fusion | flops 4147200 | bytes 4401664
  48.1 2.8 fusion.20
  50.9 19.4 %reshape.99 = bf16[4050,2304]{1,0:T(8,128)(2,1)} reshape(bf16[90,45,2304]{2,1,0:T(8,128)(2,1)} %fusion.20) | data formatting | bytes 37324800 | tf_op jit(solution)/shard_map/reshape | solution.py:36
  70.3 24.9 %copy.7 = bf16[4050,2304]{0,1:T(8,128)(2,1)} copy(bf16[4050,2304]{1,0:T(8,128)(2,1)} %reshape.99) | data formatting | bytes 37324800 | tf_op jit(solution)/shard_map/reshape | solution.py:36
  95.2 10.4 %fusion.24 = f32[3,3,256,256]{3,2,1,0:T(8,128)} fusion(bf16[3,3,256,4050]{3,2,1,0:T(8,128)(2,1)} %bitcast.46, bf16[4050,256,1,1]{1,0,2,3:T(8,128)(2,1)S(1)} %copy-done.3), kind=kOutput, calls=%fused_computation.43 | convolution fusion | flops 4777574400 | bytes 23095296 | tf_op jit(solution)/shard_map/dot_general | solution.py:72
  106.5 1.9 collective-permute-start.6
  110.3 2.8 collective-permute-done.5
  113.1 1.8 constant_dynamic-update-slice_fusion.5
  114.9 57.1 %all-reduce.2.cloned.1.call-done = f32[3,3,256,256]{3,2,1,0:T(8,128)} async-done(((f32[3,3,256,256]{3,2,1,0:T(8,128)}), f32[3,3,256,256]{3,2,1,0:T(8,128)}) %all-reduce.2.cloned.1.call-update) | async-done | bytes 2359312 | tf_op jit(solution)/shard_map/psum | solution.py:99
  174.3 3.5 %collective-permute-start.8 = (bf16[92,1,256]{2,1,0:T(2,128)(2,1)}, bf16[92,1,256]{2,1,0:T(2,128)(2,1)S(1)}, u32[]{:S(2)}, u32[]{:S(2)}) collective-permute-start(bf16[92,1,256]{2,1,0:T(2,128)(2,1)} %get-tuple-element.32), channel_id=1, source_target_pairs={{1,0},{2,1},{3,2},{4,3},{5,4},{6,5},{7,6},{0,7},{9,8},{10,9},{11,1... | collective-permute-start | bytes 141320 | tf_op jit(solution)/shard_map/ppermute | solution.py:17
  177.8 2.0 fusion.71
  182.2 2.3 pad_maximum_fusion.1
  186.9 2.7 fusion.5
  189.6 2.7 fusion.19
  192.4 3.6 %fusion.18 = bf16[90,45,2304]{2,1,0:T(8,128)(2,1)} fusion(bf16[90,45,2304]{2,1,0:T(8,128)(2,1)} %fusion.19, bf16[92,45,256]{2,1,0:T(8,128)(2,1)S(1)} %constant_dynamic-update-slice_fusion.4, bf16[92,1,256]{2,1,0:T(2,128)(2,1)} %collective-permute-done.7), kind=kLoop, calls=%fused_computation.32 | loop fusion | flops 4147200 | bytes 4425728
  197.6 3.0 %fusion.17 = bf16[90,45,2304]{2,1,0:T(8,128)(2,1)} fusion(bf16[90,45,2304]{2,1,0:T(8,128)(2,1)} %constant_dynamic-update-slice_fusion.7, bf16[92,1,256]{2,1,0:T(2,128)(2,1)S(1)} %collective-permute-done.8, bf16[92,45,256]{2,1,0:T(8,128)(2,1)S(1)} %constant_dynamic-update-slice_fusion.4), kind=kLoop, calls=%fused_computation.30 | loop fusion | flops 4147200 | bytes 4378624
  202.2 2.7 fusion.1
  204.9 2.8 fusion.16
  207.7 16.1 %collective-permute-done.10 = f32[3,3,256,256]{3,2,1,0:T(8,128)} collective-permute-done((f32[3,3,256,256]{3,2,1,0:T(8,128)}, f32[3,3,256,256]{3,2,1,0:T(8,128)}, u32[]{:S(2)}, u32[]{:S(2)}) %collective-permute-start.10) | collective-permute-done | bytes 2359328 | tf_op jit(solution)/shard_map/ppermute | solution.py:102
  223.7 2.0 add.24
  227.2 9.8 %fusion.72 = f32[90,45,256]{2,1,0:T(8,128)S(1)} fusion(bf16[90,45,2304]{2,1,0:T(8,128)(2,1)} %fusion.16, bf16[2304,256,1]{1,0,2:T(8,128)(2,1)S(1)} %bitcast.50), kind=kOutput, calls=%fused_computation.114 | convolution fusion | flops 4777574400 | bytes 23989248 | tf_op jit(solution)/shard_map/dot_general | solution.py:88
  239.2 11.5 %convolution_convert_fusion = bf16[90,45,256]{2,1,0:T(8,128)(2,1)} fusion(bf16[90,45,2304]{2,1,0:T(8,128)(2,1)} %fusion.20, bf16[2304,256,1]{1,0,2:T(8,128)(2,1)S(1)} %bitcast.49), kind=kOutput, calls=%fused_computation.45 | convolution fusion | flops 4778611200 | bytes 21915648 | tf_op jit(solution)/shard_map/dot_general | solution.py:69
  250.7 25.6 %collective-permute-done.11 = f32[3,3,256,256]{3,2,1,0:T(8,128)S(1)} collective-permute-done((f32[3,3,256,256]{3,2,1,0:T(8,128)S(1)}, f32[3,3,256,256]{3,2,1,0:T(8,128)S(1)}, u32[]{:S(2)}, u32[]{:S(2)}) %collective-permute-start.11) | collective-permute-done | bytes 2359328 | tf_op jit(solution)/shard_map/ppermute | solution.py:102
  (65 shorter events, 30.4 us)
Async XLA Ops:
  7.2 164.9 %all-reduce.2.cloned.1.call-start = ((), (), s32[]{:S(2)}) async-start(), calls=%async_computation | async-start | bytes 4718592 | tf_op jit(solution)/shard_map/psum | solution.py:99
  8.0 5.7 %collective-permute-start = (bf16[1,45,256]{2,1,0:T(8,128)(2,1)S(1)}, bf16[1,45,256]{2,1,0:T(8,128)(2,1)S(1)}, u32[]{:S(2)}, u32[]{:S(2)}) collective-permute-start(bf16[1,45,256]{2,1,0:T(8,128)(2,1)S(1)} %get-tuple-element.38), channel_id=1, source_target_pairs={{0,8},{8,16},{16,24},{24,0},{1,9},{9,17},{17,25},{25,1},{2,10},{10... | collective-permute-start | bytes 69128 | tf_op jit(solution)/shard_map/ppermute | solution.py:15
  10.9 4.5 %collective-permute-start.1 = (bf16[1,45,256]{2,1,0:T(8,128)(2,1)S(1)}, bf16[1,45,256]{2,1,0:T(8,128)(2,1)S(1)}, u32[]{:S(2)}, u32[]{:S(2)}) collective-permute-start(bf16[1,45,256]{2,1,0:T(8,128)(2,1)S(1)} %get-tuple-element.37), channel_id=1, source_target_pairs={{8,0},{16,8},{24,16},{0,24},{9,1},{17,9},{25,17},{1,25},{10,2},{18... | collective-permute-start | bytes 69128 | tf_op jit(solution)/shard_map/ppermute | solution.py:17
  15.7 7.6 %collective-permute-start.2 = (bf16[92,1,256]{2,1,0:T(2,128)(2,1)S(1)}, bf16[92,1,256]{2,1,0:T(2,128)(2,1)S(1)}, u32[]{:S(2)}, u32[]{:S(2)}) collective-permute-start(bf16[92,1,256]{2,1,0:T(2,128)(2,1)S(1)} %get-tuple-element.33), channel_id=1, source_target_pairs={{0,1},{1,2},{2,3},{3,4},{4,5},{5,6},{6,7},{7,0},{8,9},{9,10},{10,1... | collective-permute-start | bytes 141320 | tf_op jit(solution)/shard_map/ppermute | solution.py:15
  15.7 7.5 %collective-permute-start.3 = (bf16[92,1,256]{2,1,0:T(2,128)(2,1)S(1)}, bf16[92,1,256]{2,1,0:T(2,128)(2,1)S(1)}, u32[]{:S(2)}, u32[]{:S(2)}) collective-permute-start(bf16[92,1,256]{2,1,0:T(2,128)(2,1)S(1)} %get-tuple-element.34), channel_id=1, source_target_pairs={{1,0},{2,1},{3,2},{4,3},{5,4},{6,5},{7,6},{0,7},{9,8},{10,9},{11,1... | collective-permute-start | bytes 141320 | tf_op jit(solution)/shard_map/ppermute | solution.py:17
  23.3 5.4 %collective-permute-start.4 = (bf16[2,47,256]{2,1,0:T(8,128)(2,1)S(1)}, bf16[2,47,256]{2,1,0:T(8,128)(2,1)S(1)}, u32[]{:S(2)}, u32[]{:S(2)}) collective-permute-start(bf16[2,47,256]{2,1,0:T(8,128)(2,1)S(1)} %fusion.54), channel_id=1, source_target_pairs={{0,4},{1,5},{2,6},{3,7},{4,0},{5,1},{6,2},{7,3},{8,12},{9,13},{10,... | collective-permute-start | bytes 144392 | tf_op jit(solution)/shard_map/ppermute | solution.py:27
  36.0 2.9 %copy-start.1 = (bf16[90,45,256]{2,1,0:T(8,128)(2,1)S(1)}, bf16[90,45,256]{2,1,0:T(8,128)(2,1)}, u32[]{:S(2)}) copy-start(bf16[90,45,256]{2,1,0:T(8,128)(2,1)} %param.7) | copy-start | bytes 6220804
  70.3 24.9 %copy-start.3 = (bf16[4050,256,1,1]{1,0,2,3:T(8,128)(2,1)S(1)}, bf16[4050,256,1,1]{1,0,2,3:T(8,128)(2,1)}, u32[]{:S(2)}) copy-start(bf16[4050,256,1,1]{1,0,2,3:T(8,128)(2,1)} %reshape.103) | copy-start | bytes 6220804
  105.6 2.9 %copy-start.6 = (bf16[3,3,256,256]{3,2,1,0:T(8,128)(2,1)S(1)}, bf16[3,3,256,256]{3,2,1,0:T(8,128)(2,1)}, u32[]{:S(2)}) copy-start(bf16[3,3,256,256]{3,2,1,0:T(8,128)(2,1)} %param.8) | copy-start | bytes 3538948
  106.5 8.4 %collective-permute-start.6 = (bf16[1,45,256]{2,1,0:T(8,128)(2,1)S(1)}, bf16[1,45,256]{2,1,0:T(8,128)(2,1)S(1)}, u32[]{:S(2)}, u32[]{:S(2)}) collective-permute-start(bf16[1,45,256]{2,1,0:T(8,128)(2,1)S(1)} %get-tuple-element.35), channel_id=1, source_target_pairs={{8,0},{16,8},{24,16},{0,24},{9,1},{17,9},{25,17},{1,25},{10,2},{18... | collective-permute-start | bytes 69128 | tf_op jit(solution)/shard_map/ppermute | solution.py:17
  108.4 4.7 %collective-permute-start.5 = (bf16[1,45,256]{2,1,0:T(8,128)(2,1)S(1)}, bf16[1,45,256]{2,1,0:T(8,128)(2,1)S(1)}, u32[]{:S(2)}, u32[]{:S(2)}) collective-permute-start(bf16[1,45,256]{2,1,0:T(8,128)(2,1)S(1)} %get-tuple-element.36), channel_id=1, source_target_pairs={{0,8},{8,16},{16,24},{24,0},{1,9},{9,17},{17,25},{25,1},{2,10},{10... | collective-permute-start | bytes 69128 | tf_op jit(solution)/shard_map/ppermute | solution.py:15
  172.0 51.7 %collective-permute-start.10 = (f32[3,3,256,256]{3,2,1,0:T(8,128)}, f32[3,3,256,256]{3,2,1,0:T(8,128)}, u32[]{:S(2)}, u32[]{:S(2)}) collective-permute-start(f32[3,3,256,256]{3,2,1,0:T(8,128)} %all-reduce.2.cloned.1.call-done), channel_id=1, source_target_pairs={{0,8},{8,0},{16,24},{24,16},{1,9},{9,1},{17,25},{25,17},{2,10},{10... | collective-permute-start | bytes 7077896 | tf_op jit(solution)/shard_map/ppermute | solution.py:102
  174.3 7.1 %collective-permute-start.7 = (bf16[92,1,256]{2,1,0:T(2,128)(2,1)}, bf16[92,1,256]{2,1,0:T(2,128)(2,1)}, u32[]{:S(2)}, u32[]{:S(2)}) collective-permute-start(bf16[92,1,256]{2,1,0:T(2,128)(2,1)} %get-tuple-element.31), channel_id=1, source_target_pairs={{0,1},{1,2},{2,3},{3,4},{4,5},{5,6},{6,7},{7,0},{8,9},{9,10},{10,1... | collective-permute-start | bytes 141320 | tf_op jit(solution)/shard_map/ppermute | solution.py:15
  174.3 7.1 %collective-permute-start.8 = (bf16[92,1,256]{2,1,0:T(2,128)(2,1)}, bf16[92,1,256]{2,1,0:T(2,128)(2,1)S(1)}, u32[]{:S(2)}, u32[]{:S(2)}) collective-permute-start(bf16[92,1,256]{2,1,0:T(2,128)(2,1)} %get-tuple-element.32), channel_id=1, source_target_pairs={{1,0},{2,1},{3,2},{4,3},{5,4},{6,5},{7,6},{0,7},{9,8},{10,9},{11,1... | collective-permute-start | bytes 141320 | tf_op jit(solution)/shard_map/ppermute | solution.py:17
  182.1 55.0 %collective-permute-start.9 = (bf16[2,47,256]{2,1,0:T(8,128)(2,1)S(1)}, bf16[2,47,256]{2,1,0:T(8,128)(2,1)S(1)}, u32[]{:S(2)}, u32[]{:S(2)}) collective-permute-start(bf16[2,47,256]{2,1,0:T(8,128)(2,1)S(1)} %fusion.57), channel_id=1, source_target_pairs={{0,4},{1,5},{2,6},{3,7},{4,0},{5,1},{6,2},{7,3},{8,12},{9,13},{10,... | collective-permute-start | bytes 144392 | tf_op jit(solution)/shard_map/ppermute | solution.py:27
  192.4 3.6 %copy-start = (bf16[90,45,256]{2,1,0:T(8,128)(2,1)S(1)}, bf16[90,45,256]{2,1,0:T(8,128)(2,1)}, u32[]{:S(2)}) copy-start(bf16[90,45,256]{2,1,0:T(8,128)(2,1)} %param.9) | copy-start | bytes 6220804
  204.9 18.8 %copy-start.2 = (f32[3,3,256,256]{3,2,1,0:T(8,128)S(1)}, f32[3,3,256,256]{3,2,1,0:T(8,128)}, u32[]{:S(2)}) copy-start(f32[3,3,256,256]{3,2,1,0:T(8,128)} %all-reduce.2.cloned.1.call-done) | copy-start | bytes 7077892
  207.7 19.6 %copy-start.8 = (bf16[3,3,256,256]{2,3,1,0:T(8,128)(2,1)S(1)}, bf16[3,3,256,256]{2,3,1,0:T(8,128)(2,1)}, u32[]{:S(2)}) copy-start(bf16[3,3,256,256]{2,3,1,0:T(8,128)(2,1)} %rev.3) | copy-start | bytes 3538948
  225.7 50.6 %collective-permute-start.11 = (f32[3,3,256,256]{3,2,1,0:T(8,128)S(1)}, f32[3,3,256,256]{3,2,1,0:T(8,128)S(1)}, u32[]{:S(2)}, u32[]{:S(2)}) collective-permute-start(f32[3,3,256,256]{3,2,1,0:T(8,128)S(1)} %add.24), channel_id=1, source_target_pairs={{0,16},{8,24},{16,0},{24,8},{1,17},{9,25},{17,1},{25,9},{2,18},{10... | collective-permute-start | bytes 7077896 | tf_op jit(solution)/shard_map/ppermute | solution.py:102
  227.2 9.9 %copy-start.5 = (bf16[1,3,256,256]{3,2,1,0:T(8,128)(2,1)S(1)}, bf16[1,3,256,256]{3,2,1,0:T(8,128)(2,1)}, u32[]{:S(2)}) copy-start(bf16[1,3,256,256]{3,2,1,0:T(8,128)(2,1)} %get-tuple-element.40) | copy-start | bytes 1179652
  227.2 10.1 %copy-start.4 = (bf16[1,3,256,256]{3,2,1,0:T(8,128)(2,1)S(1)}, bf16[1,3,256,256]{3,2,1,0:T(8,128)(2,1)}, u32[]{:S(2)}) copy-start(bf16[1,3,256,256]{3,2,1,0:T(8,128)(2,1)} %get-tuple-element.39) | copy-start | bytes 1179652
  237.6 1.6 copy-start.7
Sparse Core Ops, SparseCore 0:
  105.7 66.2 all-reduce.1
